TPU v7x, 32 devices: a whole 2x2x4 slice. The times are simulated.
32 devices in a mesh: dp: 4 (over z), expert: 8 (over y, x, core).
Axes of the slice: x: 2, y: 2, z: 4, core: 2. Of those that a mesh axis runs over, the one named last changes fastest.
Arguments:
- inputs: bfloat16 [1024, 2048], P('expert', 'dp'), may hold values from -6 to 6
- out_grad: bfloat16 [1024, 2048], P('expert', 'dp'), may hold values from -6 to 6
- gate_probs: float32 [1024, 2], P('expert'), may hold values from 0.1 to 1
- expert_ids: int32 [1024, 2], P('expert'), may hold values from 0 to 7, all different within a row; in each aligned block of 128 rows (0 to 127, 128 to 255, ...) at most 48 rows name the same one
- gate_proj: bfloat16 [8, 2048, 2304], P('expert', None, 'dp'), may hold values from -0.125 to 0.125
- down_proj: bfloat16 [8, 2304, 2048], P('expert', 'dp'), may hold values from -0.125 to 0.125
Outputs:
- layer_out: bfloat16 [1024, 2048], P('expert', 'dp')
- in_grad: bfloat16 [1024, 2048], P('expert', 'dp')
- prob_grad: float32 [1024, 2], P('expert')
Inputs may be any that keep to these rules, and one draw needn't show every extreme that they name: `expert_ids`: each token names two different experts. Within each home group of 128 tokens no expert is named by more than 48 tokens, and in every draw some group names some expert exactly 48 times.
All inputs are finite; a program needn't handle non-finite values.
Results may differ from a plain program's by a relative error of at most 0.012.
Values may be sent and summed in bfloat16 or wider, within the bound.
A program may use at most 64 MiB of HBM per device.

v0:
```python
import jax
import jax.numpy as jnp
from jax import lax
from jax.sharding import PartitionSpec as P


def slot_tables(expert_ids, experts, capacity):
    flat = expert_ids.reshape(-1)
    copies = flat.shape[0]
    onehot = (flat[:, None] == jnp.arange(experts, dtype=jnp.int32)[None, :]).astype(jnp.int32)
    before = jnp.cumsum(onehot, axis=0) - onehot
    position = jnp.sum(before * onehot, axis=1)
    target = flat * capacity + position
    filler = jnp.full((experts * capacity,), copies, jnp.int32)
    slot_copy = filler.at[target].set(jnp.arange(copies, dtype=jnp.int32))
    return (target, slot_copy)


def with_zero_row(values):
    return jnp.concatenate([values, jnp.zeros((1, values.shape[1]), values.dtype)], axis=0)


def contract_last(left, right):
    return lax.dot_general(
        left, right, (((1,), (1,)), ((), ())), preferred_element_type=jnp.float32
    )


def per_device(inputs, out_grad, gate_probs, expert_ids, gate_proj, down_proj):
    experts = lax.axis_size("expert")
    local_tokens = inputs.shape[0]
    columns = inputs.shape[1]
    capacity = 3 * local_tokens // experts
    copies = 2 * local_tokens
    rows = experts * capacity
    w_gate = gate_proj[0]
    w_down = down_proj[0]
    width = w_gate.shape[0]
    target, slot_copy = slot_tables(expert_ids, experts, capacity)
    slot_token = jnp.where(slot_copy < copies, slot_copy // 2, local_tokens)
    prob_pad = jnp.concatenate([gate_probs.reshape(-1), jnp.zeros((1,), jnp.float32)])
    slot_prob = prob_pad[slot_copy][:, None]
    home_x, home_dy = (
        lax.all_gather(inputs, "dp", axis=1, tiled=True),
        lax.all_gather(out_grad, "dp", axis=1, tiled=True),
    )
    send_x = with_zero_row(home_x)[slot_token].reshape(experts, capacity, width)
    send_g = (slot_prob * with_zero_row(home_dy)[slot_token].astype(jnp.float32)).astype(
        jnp.bfloat16
    )
    send_g = send_g.reshape(experts, capacity, width)
    recv_x, recv_g = (
        lax.all_to_all(send_x, "expert", split_axis=0, concat_axis=0, tiled=True),
        lax.all_to_all(send_g, "expert", split_axis=0, concat_axis=0, tiled=True),
    )
    x_rows = recv_x.reshape(rows, width)
    grad_rows = recv_g.reshape(rows, width)
    pre_gate = jnp.dot(x_rows, w_gate, preferred_element_type=jnp.float32)
    back = contract_last(grad_rows, w_down)
    sig = jax.nn.sigmoid(pre_gate)
    hidden = (pre_gate * sig).astype(jnp.bfloat16)
    gate_term = (back * sig * (1.0 + pre_gate * (1.0 - sig))).astype(jnp.bfloat16)
    out_part = jnp.dot(hidden, w_down, preferred_element_type=jnp.float32).reshape(
        experts, capacity, width
    )
    in_part = contract_last(gate_term, w_gate).reshape(experts, capacity, width)
    out_sum, in_sum = (
        lax.psum_scatter(
            out_part.astype(jnp.bfloat16), "dp", scatter_dimension=2, tiled=True
        ).astype(jnp.float32),
        lax.psum_scatter(
            in_part.astype(jnp.bfloat16), "dp", scatter_dimension=2, tiled=True
        ).astype(jnp.float32),
    )
    slot_out, slot_in = (
        lax.all_to_all(
            out_sum.astype(jnp.bfloat16), "expert", split_axis=0, concat_axis=0, tiled=True
        ),
        lax.all_to_all(
            in_sum.astype(jnp.bfloat16), "expert", split_axis=0, concat_axis=0, tiled=True
        ),
    )
    out_copy = (
        slot_out.reshape(rows, columns)[target]
        .reshape(local_tokens, 2, columns)
        .astype(jnp.float32)
    )
    grad_copy = (
        slot_in.reshape(rows, columns)[target].reshape(local_tokens, 2, columns).astype(jnp.float32)
    )
    layer_out = jnp.sum(gate_probs[:, :, None] * out_copy, axis=1).astype(jnp.bfloat16)
    in_grad = jnp.sum(grad_copy, axis=1).astype(jnp.bfloat16)
    prob_part = jnp.sum(out_grad.astype(jnp.float32)[:, None, :] * out_copy, axis=2)
    prob_grad = lax.psum(prob_part, "dp")
    return (layer_out, in_grad, prob_grad)


def solution(mesh):
    placed = (
        P("expert", "dp"),
        P("expert", "dp"),
        P("expert", None),
        P("expert", None),
        P("expert", None, "dp"),
        P("expert", "dp", None),
    )
    return jax.shard_map(
        per_device,
        mesh=mesh,
        in_specs=placed,
        out_specs=(P("expert", "dp"), P("expert", "dp"), P("expert", None)),
        check_vma=False,
    )
```

profile of v0, /device:TPU:0, one launch (start us, length us, event | category | flops | bytes accessed | tf_op | source)
XLA Modules:
  0.0 203.4 jit_solution(9731457621306514366)
XLA Ops:
  7.2 0.8 broadcast_multiply_fusion
  8.0 0.8 copy.21
  9.1 17.6 %all_gather.6 = bf16[128,2048]{1,0:T(8,128)(2,1)S(1)} all-gather(bf16[128,512]{1,0:T(8,128)(2,1)} %param.6), channel_id=1, replica_groups=mesh['dp'=4,'expert'=8] {'dp'}, dimensions={1}, use_global_device_ids=true | all-gather | bytes 655360 | tf_op jit(solution)/shard_map/all_gather | solution.py:44
  26.9 0.6 reduce-window.6
  27.9 1.4 scatter_custom_fusion
  29.4 3.1 %gather_fusion = bf16[384,2048]{1,0:T(8,128)(2,1)} fusion(bf16[129,2048]{1,0:T(8,128)(2,1)S(1)} %concatenate.9, s32[1024]{0:T(1024)S(1)} %pad_clamp_fusion.2), kind=kCustom, calls=%fused_computation | custom fusion | bytes 3147264 | tf_op jit(solution)/shard_map/gather | solution.py:47
  32.5 4.4 %all-to-all-start = ((bf16[8,48,2048]{2,1,0:T(8,128)(2,1)}), bf16[8,48,2048]{2,1,0:T(8,128)(2,1)}, u32[]{:S(2)}, u32[]{:S(2)}) async-start(bf16[8,48,2048]{2,1,0:T(8,128)(2,1)} %bitcast.46), calls=%async_computation | async-start | bytes 3145728 | tf_op jit(solution)/shard_map/all_to_all | solution.py:53
  37.1 20.9 %all-to-all-done = bf16[8,48,2048]{2,1,0:T(8,128)(2,1)} async-done(((bf16[8,48,2048]{2,1,0:T(8,128)(2,1)}), bf16[8,48,2048]{2,1,0:T(8,128)(2,1)}, u32[]{:S(2)}, u32[]{:S(2)}) %all-to-all-start) | async-done | bytes 1572896 | tf_op jit(solution)/shard_map/all_to_all | solution.py:53
  58.0 3.7 %multiply_convert_fusion = (bf16[384,576]{0,1:T(8,128)(2,1)S(1)}, f32[384,576]{0,1:T(8,128)}) fusion(bf16[384,2048]{1,0:T(8,128)(2,1)} %bitcast.5, bf16[1,2048,576]{1,2,0:T(8,128)(2,1)S(1)} %copy-done), kind=kOutput, calls=%fused_computation.19 | convolution fusion | flops 907075584 | bytes 5259264 | tf_op jit(solution)/shard_map/dot_general | solution.py:58
  61.7 0.3 copy.23
  61.9 4.2 %convolution_convert_fusion.1 = bf16[8,48,2048]{2,1,0:T(8,128)(2,1)} fusion(bf16[8,48,576]{2,1,0:T(8,128)(2,1)S(1)} %bitcast.48, bf16[1,576,2048]{2,1,0:T(8,128)(2,1)} %param.11), kind=kOutput, calls=%fused_computation.9 | convolution fusion | flops 906756096 | bytes 4374528 | tf_op jit(solution)/shard_map/dot_general | solution.py:63
  66.2 0.8 copy-done.2
  67.1 21.7 %all_gather.7 = bf16[128,2048]{1,0:T(8,128)(2,1)S(1)} all-gather(bf16[128,512]{1,0:T(8,128)(2,1)S(1)} %copy-done.2), channel_id=1, replica_groups=mesh['dp'=4,'expert'=8] {'dp'}, dimensions={1}, use_global_device_ids=true | all-gather | bytes 655360 | tf_op jit(solution)/shard_map/all_gather | solution.py:45
  88.8 3.1 %gather_fusion.3 = bf16[384,2048]{1,0:T(8,128)(2,1)} fusion(bf16[129,2048]{1,0:T(8,128)(2,1)S(1)} %concatenate.11, s32[1024]{0:T(1024)S(1)} %pad_clamp_fusion.2), kind=kCustom, calls=%fused_computation.3 | custom fusion | bytes 3147264 | tf_op jit(solution)/shard_map/gather | solution.py:48
  92.1 2.8 %gather_fusion.2 = f32[384]{0:T(512)S(1)} fusion(f32[257]{0:T(512)S(1)} %pad_maximum_fusion, s32[1024]{0:T(1024)S(1)} %pad_clamp_fusion), kind=kCustom, calls=%fused_computation.2 | custom fusion | bytes 4608 | tf_op jit(solution)/shard_map/gather | solution.py:42
  95.0 1.8 fusion
  96.9 23.9 %all_to_all.20 = bf16[8,48,2048]{2,1,0:T(8,128)(2,1)S(1)} all-to-all(bf16[8,48,2048]{2,1,0:T(8,128)(2,1)S(1)} %fusion), channel_id=1, replica_groups=mesh['dp'=4,'expert'=8] {'expert'}, dimensions={0} | all-to-all | bytes 3145728 | tf_op jit(solution)/shard_map/all_to_all | solution.py:54
  120.8 2.3 %fusion.13 = bf16[384,576]{0,1:T(8,128)(2,1)} fusion(bf16[384,2048]{1,0:T(8,128)(2,1)S(1)} %bitcast.47, bf16[1,576,2048]{2,1,0:T(8,128)(2,1)S(1)} %copy-done.4, f32[384,576]{0,1:T(8,128)S(1)} %copy-done.5), kind=kOutput, calls=%fused_computation.18 | convolution fusion | flops 907960320 | bytes 5259264 | tf_op jit(solution)/shard_map/dot_general | solution.py:24
  123.1 1.3 copy.25
  124.3 2.5 %convolution_convert_fusion = bf16[8,48,2048]{2,1,0:T(8,128)(2,1)} fusion(bf16[8,48,576]{2,1,0:T(8,128)(2,1)S(1)} %bitcast.49, bf16[1,2048,576]{1,2,0:T(8,128)(2,1)S(1)} %copy-done), kind=kOutput, calls=%fused_computation.8 | convolution fusion | flops 906756096 | bytes 4374528 | tf_op jit(solution)/shard_map/dot_general | solution.py:24
  126.9 3.5 %all-to-all-start.1 = ((bf16[8,48,512]{2,1,0:T(8,128)(2,1)}), bf16[8,48,512]{2,1,0:T(8,128)(2,1)S(1)}, u32[]{:S(2)}, u32[]{:S(2)}) async-start(bf16[8,48,512]{2,1,0:T(8,128)(2,1)} %reduce-scatter.3.cloned.1.call-done), calls=%async_computation.2 | async-start | bytes 786432 | tf_op jit(solution)/shard_map/all_to_all | solution.py:76
  130.4 30.5 %reduce-scatter.5.cloned.1.call-done = bf16[8,48,512]{2,1,0:T(8,128)(2,1)} async-done(((bf16[8,48,2048]{2,1,0:T(8,128)(2,1)}), bf16[8,48,512]{2,1,0:T(8,128)(2,1)}) %reduce-scatter.5.cloned.1.call-update) | async-done | bytes 393232 | tf_op jit(solution)/shard_map/reduce_scatter | solution.py:71
  160.9 3.7 %all-to-all-start.3 = ((bf16[8,48,512]{2,1,0:T(8,128)(2,1)}), bf16[8,48,512]{2,1,0:T(8,128)(2,1)S(1)}, u32[]{:S(2)}, u32[]{:S(2)}) async-start(bf16[8,48,512]{2,1,0:T(8,128)(2,1)} %reduce-scatter.5.cloned.1.call-done), calls=%async_computation.5 | async-start | bytes 786432 | tf_op jit(solution)/shard_map/all_to_all | solution.py:79
  164.5 0.7 convert_element_type.64
  165.3 1.2 gather_fusion.1
  166.4 1.1 reshape.110
  167.5 5.3 %all-to-all-done.3 = bf16[8,48,512]{2,1,0:T(8,128)(2,1)S(1)} async-done(((bf16[8,48,512]{2,1,0:T(8,128)(2,1)}), bf16[8,48,512]{2,1,0:T(8,128)(2,1)S(1)}, u32[]{:S(2)}, u32[]{:S(2)}) %all-to-all-start.3) | async-done | bytes 393248 | tf_op jit(solution)/shard_map/all_to_all | solution.py:79
  172.9 1.2 gather_fusion.4
  174.1 1.3 reduce_sum.44
  175.5 2.7 %multiply_reduce_fusion = (f32[128,2]{1,0:T(8,128)S(1)}, bf16[128,512]{1,0:T(8,128)(2,1)}) fusion(f32[128,2,512]{2,1,0:T(2,128)} %reshape.110, f32[128,512]{1,0:T(8,128)S(1)} %copy-done.1, f32[128,2]{1,0:T(8,128)S(1)} %copy.19), kind=kLoop, calls=%fused_computation.21 | loop fusion | flops 458496 | bytes 919552 | tf_op jit(solution)/shard_map/reduce_sum | solution.py:93
  178.2 17.8 %psum.7 = f32[128,2]{1,0:T(8,128)S(1)} all-reduce(f32[128,2]{1,0:T(8,128)S(1)} %get-tuple-element.6), channel_id=1, replica_groups=mesh['dp'=4,'expert'=8] {'dp'}, use_global_device_ids=true, to_apply=%region_9.10 | all-reduce | flops 256 | bytes 2048 | tf_op jit(solution)/shard_map/psum | solution.py:94
  196.0 0.6 copy.26
  (39 shorter events, 1.6 us)
Async XLA Ops:
  7.2 50.8 %copy-start = (bf16[1,2048,576]{1,2,0:T(8,128)(2,1)S(1)}, bf16[1,2048,576]{1,2,0:T(8,128)(2,1)}, u32[]{:S(2)}) copy-start(bf16[1,2048,576]{1,2,0:T(8,128)(2,1)} %param.10) | copy-start | bytes 7077892
  32.5 4.5 %copy-start.3 = (f32[128,2]{0,1:T(2,128)S(1)}, f32[128,2]{0,1:T(2,128)}, u32[]{:S(2)}) copy-start(f32[128,2]{0,1:T(2,128)} %param.8) | copy-start | bytes 3076
  32.5 25.5 %all-to-all-start = ((bf16[8,48,2048]{2,1,0:T(8,128)(2,1)}), bf16[8,48,2048]{2,1,0:T(8,128)(2,1)}, u32[]{:S(2)}, u32[]{:S(2)}) async-start(bf16[8,48,2048]{2,1,0:T(8,128)(2,1)} %bitcast.46), calls=%async_computation | async-start | bytes 3145728 | tf_op jit(solution)/shard_map/all_to_all | solution.py:53
  36.9 90.0 %reduce-scatter.3.cloned.1.call-start = ((), (), s32[]{:S(2)}) async-start(), calls=%async_computation.6 | async-start | bytes 1966080 | tf_op jit(solution)/shard_map/reduce_scatter | solution.py:68
  66.1 0.9 copy-start.2
  66.2 94.7 %reduce-scatter.5.cloned.1.call-start = ((), (), s32[]{:S(2)}) async-start(), calls=%async_computation.7 | async-start | bytes 1966080 | tf_op jit(solution)/shard_map/reduce_scatter | solution.py:71
  95.0 25.8 %copy-start.5 = (f32[384,576]{0,1:T(8,128)S(1)}, f32[384,576]{0,1:T(8,128)}, u32[]{:S(2)}) copy-start(f32[384,576]{0,1:T(8,128)} %get-tuple-element.11) | copy-start | bytes 2654212
  96.8 23.9 %copy-start.4 = (bf16[1,576,2048]{2,1,0:T(8,128)(2,1)S(1)}, bf16[1,576,2048]{2,1,0:T(8,128)(2,1)}, u32[]{:S(2)}) copy-start(bf16[1,576,2048]{2,1,0:T(8,128)(2,1)} %param.11) | copy-start | bytes 7077892
  126.9 33.9 %all-to-all-start.1 = ((bf16[8,48,512]{2,1,0:T(8,128)(2,1)}), bf16[8,48,512]{2,1,0:T(8,128)(2,1)S(1)}, u32[]{:S(2)}, u32[]{:S(2)}) async-start(bf16[8,48,512]{2,1,0:T(8,128)(2,1)} %reduce-scatter.3.cloned.1.call-done), calls=%async_computation.2 | async-start | bytes 786432 | tf_op jit(solution)/shard_map/all_to_all | solution.py:76
  160.9 12.0 %all-to-all-start.3 = ((bf16[8,48,512]{2,1,0:T(8,128)(2,1)}), bf16[8,48,512]{2,1,0:T(8,128)(2,1)S(1)}, u32[]{:S(2)}, u32[]{:S(2)}) async-start(bf16[8,48,512]{2,1,0:T(8,128)(2,1)} %reduce-scatter.5.cloned.1.call-done), calls=%async_computation.5 | async-start | bytes 786432 | tf_op jit(solution)/shard_map/all_to_all | solution.py:79
  172.9 2.6 %copy-start.1 = (f32[128,512]{1,0:T(8,128)S(1)}, f32[128,512]{1,0:T(8,128)}, u32[]{:S(2)}) copy-start(f32[128,512]{1,0:T(8,128)} %convert_element_type.64) | copy-start | bytes 786436
Sparse Core Ops, SparseCore 0:
  66.3 39.6 reduce-scatter.2
  127.0 33.7 reduce-scatter.4
where the time goes:
time: 204 us; the launch traced here: 203 us
  blocking collectives  81 us (40%)
  waiting for transfers between devices  56.7 us (28%)
  local copies, waits for them, and re-layouts  18.9 us (9%)
  between operations  14.2 us (7%)
  matrix products  12.7 us (6%)
  starting transfers between devices  11.6 us (6%)
  other arithmetic  8.2 us (4%)
    reduce_scatter x1, waiting for transfers between devices, per_device(): lax.psum_scatter(in_part.astype(jnp.bfloat16), 'dp', scatter_dimension=2,...  30.5 us
    all_to_all x1, blocking collectives, per_device(): lax.all_to_all(send_g, 'expert', split_axis=0, concat_axis=0, tiled=True)  23.9 us
    all_gather x1, blocking collectives, per_device(): lax.all_gather(out_grad, 'dp', axis=1, tiled=True)  21.7 us
    all_to_all x1, waiting for transfers between devices, per_device(): lax.all_to_all(send_x, 'expert', split_axis=0, concat_axis=0, tiled=True)  20.9 us
    psum x1, blocking collectives, per_device(): prob_grad = lax.psum(prob_part, 'dp')  17.8 us
    all_gather x1, blocking collectives, per_device(): lax.all_gather(inputs, 'dp', axis=1, tiled=True)  17.6 us
    all_to_all x1, waiting for transfers between devices, per_device(): lax.all_to_all(in_sum.astype(jnp.bfloat16), 'expert', split_axis=0, conca...  5.33 us
    dot_general x2, matrix products, contract_last(): lax.dot_general(left, right, (((1,), (1,)), ((), ())), preferred_element_...  4.82 us
  transfers between devices with their start and end apart: 5, of which 3 were waited for; matrix products, arithmetic and copies ran while one was open for 8% of the time, Pallas kernels for 0%

commit v1 on v0

v1 whole, which is shorter than its diff:
```python
import functools

import jax
import jax.numpy as jnp
from jax import lax
from jax.experimental import pallas as pl
from jax.experimental.pallas import tpu as pltpu
from jax.sharding import PartitionSpec as P

MESH = pl.DeviceIdType.MESH
LANES = 128


def flip(a, b, size):
    out, bit = 0, 1
    while bit < size:
        out = out + ((a // bit + b // bit) % 2) * bit
        bit *= 2
    return out


def nt_dot(left, right):
    return lax.dot_general(
        left, right, (((1,), (1,)), ((), ())), preferred_element_type=jnp.float32
    )


def nn_dot(left, right):
    return jnp.dot(left, right, preferred_element_type=jnp.float32)


def moe_kernel(
    parts, experts, cap,
    x_ref, dy_ref, p_ref, id_ref, wg_hbm, wd_hbm,
    lo_ref, ig_ref, pg_ref,
    wg, wd, home, pick0, pick1, spread, weight,
    send, recv, pre, back, hid, gterm, rsend, rrecv,
    part, gathered, own, pacc, psend, precv,
    w_sem, ag_send, ag_recv, loc_sem, a_send, a_recv, rloc_sem, r_send, r_recv,
    s_send, s_recv, p_send, p_recv,
):
    z = lax.axis_index("dp")
    me = lax.axis_index("expert")
    tokens, cols = x_ref.shape
    rows = experts * cap
    bf16, f32 = jnp.bfloat16, jnp.float32

    load_g = pltpu.make_async_copy(wg_hbm.at[0], wg, w_sem.at[0])
    load_d = pltpu.make_async_copy(wd_hbm.at[0], wd, w_sem.at[1])
    load_g.start()
    load_d.start()

    barrier = pltpu.get_barrier_semaphore()

    @pl.loop(1, parts)
    def _(i):
        pl.semaphore_signal(
            barrier, inc=1, device_id={"dp": flip(z, i, parts)}, device_id_type=MESH
        )

    @pl.loop(1, experts)
    def _(j):
        pl.semaphore_signal(
            barrier, inc=1, device_id={"expert": flip(me, j, experts)}, device_id_type=MESH
        )

    ids = id_ref[...]
    probs = p_ref[...]
    id0, id1 = ids[:, 0:1], ids[:, 1:2]
    p0, p1 = probs[:, 0:1], probs[:, 1:2]
    lane = lax.broadcasted_iota(jnp.int32, (tokens, LANES), 1)
    hot0 = (lane == id0).astype(f32)
    hot1 = (lane == id1).astype(f32)
    earlier = (
        lax.broadcasted_iota(jnp.int32, (tokens, tokens), 1)
        < lax.broadcasted_iota(jnp.int32, (tokens, tokens), 0)
    ).astype(f32)
    count = nn_dot(earlier.astype(bf16), (hot0 + hot1).astype(bf16))
    pos0 = jnp.sum(count * hot0, axis=1, keepdims=True)
    pos1 = jnp.sum(count * hot1, axis=1, keepdims=True)
    slot = lax.broadcasted_iota(jnp.int32, (tokens, rows), 1)
    t0 = (slot == id0 * cap + pos0.astype(jnp.int32)).astype(f32)
    t1 = (slot == id1 * cap + pos1.astype(jnp.int32)).astype(f32)
    pick0[...] = t0.astype(bf16)
    pick1[...] = t1.astype(bf16)
    spread[...] = jnp.transpose(t0 + t1).astype(bf16)
    weight[...] = jnp.sum(jnp.transpose(t0 * p0 + t1 * p1), axis=1, keepdims=True)

    home[z, 0] = x_ref[...]
    home[z, 1] = dy_ref[...]
    pre[...] = jnp.zeros_like(pre)
    back[...] = jnp.zeros_like(back)
    pacc[...] = jnp.zeros_like(pacc)

    pl.semaphore_wait(barrier, parts - 1 + experts - 1)

    def to_home(i):
        peer = flip(z, i, parts)
        return pltpu.make_async_remote_copy(
            src_ref=home.at[z], dst_ref=home.at[z],
            send_sem=ag_send, recv_sem=ag_recv.at[z],
            device_id={"dp": peer}, device_id_type=MESH,
        )

    @pl.loop(1, parts)
    def _(i):
        to_home(i).start()

    def exchange(source, target, chunk, send_sem, recv_sem, local_sem):
        @pl.loop(1, experts)
        def _(j):
            peer = flip(me, experts - j, experts)
            pltpu.make_async_remote_copy(
                src_ref=source.at[chunk, peer], dst_ref=target.at[chunk, me],
                send_sem=send_sem, recv_sem=recv_sem.at[chunk],
                device_id={"expert": peer}, device_id_type=MESH,
            ).start()
        pltpu.make_async_copy(
            source.at[chunk, me], target.at[chunk, me], local_sem.at[chunk]
        ).start()

    def exchanged(source, target, chunk, send_sem, recv_sem, local_sem):
        pltpu.make_async_copy(
            source.at[chunk, me], target.at[chunk, me], local_sem.at[chunk]
        ).wait()
        several = target.at[chunk, pl.ds(0, experts - 1)]
        pltpu.make_async_copy(several, several, recv_sem.at[chunk]).wait()

    def dispatch(chunk):
        xs = nn_dot(spread[...], home[chunk, 0]).astype(bf16)
        gs = (weight[...] * nn_dot(spread[...], home[chunk, 1])).astype(bf16)
        send[chunk, :, 0:cap] = xs.reshape(experts, cap, cols)
        send[chunk, :, cap:] = gs.reshape(experts, cap, cols)
        exchange(send, recv, chunk, a_send, a_recv, loc_sem)

    dispatch(z)

    @pl.loop(1, parts)
    def _(i):
        chunk = flip(z, i, parts)
        pltpu.make_async_copy(home.at[chunk], home.at[chunk], ag_recv.at[chunk]).wait()
        dispatch(chunk)

    load_g.wait()
    load_d.wait()

    @pl.loop(0, parts)
    def _(i):
        chunk = flip(z, i, parts)
        start = pl.multiple_of(chunk * cols, cols)
        exchanged(send, recv, chunk, a_send, a_recv, loc_sem)
        xr = recv[chunk, :, 0:cap].reshape(rows, cols)
        gr = recv[chunk, :, cap:].reshape(rows, cols)
        pre[...] += nn_dot(xr, wg[pl.ds(start, cols), :])
        back[...] += nt_dot(gr, wd[:, pl.ds(start, cols)])

    v = pre[...]
    sig = jax.nn.sigmoid(v)
    hid[...] = (v * sig).astype(bf16)
    gterm[...] = (back[...] * sig * (1.0 + v * (1.0 - sig))).astype(bf16)

    @pl.loop(1, parts + 1)
    def _(i):
        chunk = flip(z, i % parts, parts)
        start = pl.multiple_of(chunk * cols, cols)
        out = nn_dot(hid[...], wd[:, pl.ds(start, cols)]).astype(bf16)
        grad = nt_dot(gterm[...], wg[pl.ds(start, cols), :]).astype(bf16)
        rsend[chunk, :, 0:cap] = out.reshape(experts, cap, cols)
        rsend[chunk, :, cap:] = grad.reshape(experts, cap, cols)
        exchange(rsend, rrecv, chunk, r_send, r_recv, rloc_sem)

    def combine(chunk):
        exchanged(rsend, rrecv, chunk, r_send, r_recv, rloc_sem)
        out = rrecv[chunk, :, 0:cap].reshape(rows, cols)
        grad = rrecv[chunk, :, cap:].reshape(rows, cols)
        out0, out1 = nn_dot(pick0[...], out), nn_dot(pick1[...], out)
        dy = home[chunk, 1].astype(f32)
        s0 = jnp.sum(dy * out0, axis=1, keepdims=True)
        s1 = jnp.sum(dy * out1, axis=1, keepdims=True)
        pacc[...] += jnp.where(lane == 0, s0, 0.0) + jnp.where(lane == 1, s1, 0.0)
        weights = p_ref[...]
        layer = weights[:, 0:1] * out0 + weights[:, 1:2] * out1
        return layer, nn_dot(pick0[...] + pick1[...], grad)

    def to_owner(chunk):
        return pltpu.make_async_remote_copy(
            src_ref=part.at[chunk], dst_ref=gathered.at[z],
            send_sem=s_send, recv_sem=s_recv,
            device_id={"dp": chunk}, device_id_type=MESH,
        )

    @pl.loop(1, parts)
    def _(i):
        chunk = flip(z, i, parts)
        layer, grad = combine(chunk)
        part[chunk, 0] = layer.astype(bf16)
        part[chunk, 1] = grad.astype(bf16)
        to_owner(chunk).start()

    layer, grad = combine(z)
    own[0] = layer
    own[1] = grad
    psend[...] = jnp.transpose(pacc[...])[0:8]

    @pl.loop(1, parts)
    def _(i):
        pltpu.make_async_remote_copy(
            src_ref=psend, dst_ref=precv.at[z],
            send_sem=p_send, recv_sem=p_recv,
            device_id={"dp": flip(z, i, parts)}, device_id_type=MESH,
        ).start()

    others = gathered.at[pl.ds(0, parts - 1)]
    pltpu.make_async_copy(others, others, s_recv).wait()

    @pl.loop(1, parts)
    def _(i):
        other = flip(z, i, parts)
        own[...] += gathered[other].astype(f32)

    lo_ref[...] = own[0].astype(bf16)
    ig_ref[...] = own[1].astype(bf16)

    rest = precv.at[pl.ds(0, parts - 1)]
    pltpu.make_async_copy(rest, rest, p_recv).wait()
    pg_ref[...] = psend[...]

    @pl.loop(1, parts)
    def _(i):
        pg_ref[...] += precv[flip(z, i, parts)]

    sent = home.at[pl.ds(0, parts - 1)]
    pltpu.make_async_copy(sent, sent, ag_send).wait()
    pltpu.make_async_copy(others, others, s_send).wait()
    pltpu.make_async_copy(rest, rest, p_send).wait()
    several = send.at[0, pl.ds(0, experts - 1)]

    @pl.loop(0, parts)
    def _(i):
        pltpu.make_async_copy(several, several, a_send).wait()
        pltpu.make_async_copy(several, several, r_send).wait()


def per_device(inputs, out_grad, gate_probs, expert_ids, gate_proj, down_proj):
    parts = lax.axis_size("dp")
    experts = lax.axis_size("expert")
    tokens, cols = inputs.shape
    cap = -(-(3 * tokens // experts) // 16) * 16
    rows = experts * cap
    _, width, hidden = gate_proj.shape
    bf16, f32 = jnp.bfloat16, jnp.float32
    vmem = pl.BlockSpec(memory_space=pltpu.VMEM)
    hbm = pl.BlockSpec(memory_space=pl.ANY)
    dma = pltpu.SemaphoreType.DMA
    layer_out, in_grad, prob = pl.pallas_call(
        functools.partial(moe_kernel, parts, experts, cap),
        out_shape=(
            jax.ShapeDtypeStruct((tokens, cols), bf16),
            jax.ShapeDtypeStruct((tokens, cols), bf16),
            jax.ShapeDtypeStruct((8, tokens), f32),
        ),
        in_specs=[vmem, vmem, vmem, vmem, hbm, hbm],
        out_specs=(vmem, vmem, vmem),
        scratch_shapes=[
            pltpu.VMEM((width, hidden), bf16),
            pltpu.VMEM((hidden, width), bf16),
            pltpu.VMEM((parts, 2, tokens, cols), bf16),
            pltpu.VMEM((tokens, rows), bf16),
            pltpu.VMEM((tokens, rows), bf16),
            pltpu.VMEM((rows, tokens), bf16),
            pltpu.VMEM((rows, 1), f32),
            pltpu.VMEM((parts, experts, 2 * cap, cols), bf16),
            pltpu.VMEM((parts, experts, 2 * cap, cols), bf16),
            pltpu.VMEM((rows, hidden), f32),
            pltpu.VMEM((rows, hidden), f32),
            pltpu.VMEM((rows, hidden), bf16),
            pltpu.VMEM((rows, hidden), bf16),
            pltpu.VMEM((parts, experts, 2 * cap, cols), bf16),
            pltpu.VMEM((parts, experts, 2 * cap, cols), bf16),
            pltpu.VMEM((parts, 2, tokens, cols), bf16),
            pltpu.VMEM((parts, 2, tokens, cols), bf16),
            pltpu.VMEM((2, tokens, cols), f32),
            pltpu.VMEM((tokens, LANES), f32),
            pltpu.VMEM((8, tokens), f32),
            pltpu.VMEM((parts, 8, tokens), f32),
            dma((2,)), dma, dma((parts,)), dma((parts,)), dma, dma((parts,)),
            dma((parts,)), dma, dma((parts,)), dma, dma, dma, dma,
        ],
        compiler_params=pltpu.CompilerParams(
            collective_id=0, has_side_effects=True, vmem_limit_bytes=56 * 1024 * 1024
        ),
    )(inputs, out_grad, gate_probs, expert_ids, gate_proj, down_proj)
    return layer_out, in_grad, prob[:2].T


def solution(mesh):
    placed = (
        P("expert", "dp"),
        P("expert", "dp"),
        P("expert", None),
        P("expert", None),
        P("expert", None, "dp"),
        P("expert", "dp", None),
    )
    return jax.shard_map(
        per_device,
        mesh=mesh,
        in_specs=placed,
        out_specs=(P("expert", "dp"), P("expert", "dp"), P("expert", None)),
        check_vma=False,
    )
```

time: 204 us -> 103 us (0.50)
  Pallas kernels: 0 us -> 90.1 us
  blocking collectives: 81 us -> 0 us
  waiting for transfers between devices: 56.7 us -> 0 us
  between operations: 14.2 us -> 0.64 us
  matrix products: 12.7 us -> 0 us
  starting transfers between devices: 11.6 us -> 0 us
  other arithmetic: 8.2 us -> 0 us
  local copies, waits for them, and re-layouts: 18.9 us -> 11.5 us
    pallas_call x0 -> x1, Pallas kernels: none -> 90.1 us  [per_device(): pl.pallas_call(functools.partial(moe_kernel, parts, experts, cap), out_sh...]
    all_gather x2 -> x0, blocking collectives: 39.3 us -> none  [the longest x1 21.7 us: per_device(): lax.all_gather(out_grad, 'dp', axis=1, tiled=True)]
    reduce_scatter x2 -> x0, waiting for transfers between devices: 30.5 us -> none  [the longest x1 30.5 us: per_device(): lax.psum_scatter(in_part.astype(jnp.bfloat16), 'dp', scatter_dimension=2,...]
    all_to_all x3 -> x0, waiting for transfers between devices: 26.2 us -> none  [the longest x1 20.9 us: per_device(): lax.all_to_all(send_x, 'expert', split_axis=0, concat_axis=0, tiled=True)]
    all_to_all x1 -> x0, blocking collectives: 23.9 us -> none  [per_device(): lax.all_to_all(send_g, 'expert', split_axis=0, concat_axis=0, tiled=True)]
    psum x1 -> x0, blocking collectives: 17.8 us -> none  [per_device(): prob_grad = lax.psum(prob_part, 'dp')]
    dot_general x4 -> x0, matrix products: 12.7 us -> none  [the longest x2 4.82 us: contract_last(): lax.dot_general(left, right, (((1,), (1,)), ((), ())), preferred_element_...]
    all_to_all x3 -> x0, starting transfers between devices: 11.5 us -> none  [the longest x1 4.42 us: per_device(): lax.all_to_all(send_x, 'expert', split_axis=0, concat_axis=0, tiled=True)]
  transfers between devices with their start and end apart: 5 -> 0, of which waited for: 3 -> 0; matrix products, arithmetic and copies ran while one was open for 8% -> 0% of each run, Pallas kernels for 0% -> 0%
where the time goes in v1:
time: 103 us; the launch traced here: 102 us
  Pallas kernels  90.1 us (87%)
  local copies, waits for them, and re-layouts  11.5 us (11%)
    pallas_call x1, Pallas kernels, per_device(): pl.pallas_call(functools.partial(moe_kernel, parts, experts, cap), out_sh...  90.1 us
    unnamed x5, local copies, waits for them, and re-layouts  10.3 us

profile of v1, /device:TPU:0, one launch (start us, length us, event | category | flops | bytes accessed | tf_op | source)
XLA Modules:
  0.0 102.3 jit_solution(7141206353279361129)
XLA Ops:
  0.6 1.4 %copy.9.p_ref = f32[128,2]{1,0:T(8,128)} copy(f32[128,2]{0,1:T(2,128)} %param.8) | data formatting | bytes 2048 | tf_op args[2]
  2.0 1.4 %copy.10.id_ref = s32[128,2]{1,0:T(8,128)} copy(s32[128,2]{0,1:T(2,128)} %param.9) | data formatting | bytes 2048 | tf_op args[3]
  3.5 4.3 %copy.11.wg_hbm = bf16[1,2048,576]{2,1,0:T(8,128)(2,1)} copy(bf16[1,2048,576]{1,2,0:T(8,128)(2,1)} %param.10) | data formatting | bytes 4718592 | tf_op args[4]
  7.8 90.1 %shard_map.85 = (bf16[128,512]{1,0:T(8,128)(2,1)}, bf16[128,512]{1,0:T(8,128)(2,1)}, f32[8,128]{1,0:T(8,128)}) custom-call(bf16[128,512]{1,0:T(8,128)(2,1)} %x_ref.1, bf16[128,512]{1,0:T(8,128)(2,1)} %dy_ref.1, f32[128,2]{1,0:T(8,128)} %copy.9.p_ref, s32[128,2]{1,0:T(8,128)} %copy.10.id_ref, bf16[1,2048,576]{2,1,0:T(8,128)(2,1)} %copy.11.wg_hbm, ...), custom_call_target="tpu_custom_call" | custom-call | tf_op jit(solution)/shard_map/pallas_call | solution.py:255
  97.9 1.2 %slice_bitcast_fusion = f32[128,2]{0,1:T(2,128)} fusion(f32[8,128]{1,0:T(8,128)} %get-tuple-element.8), kind=kLoop, calls=%fused_computation | loop fusion | bytes 2048 | tf_op jit(solution)/shard_map/transpose | solution.py:293
  99.1 1.6 %copy.14 = bf16[128,512]{1,0:T(8,128)(2,1)} copy(bf16[128,512]{1,0:T(8,128)(2,1)} %get-tuple-element.12) | data formatting | bytes 262144
  100.7 1.6 %copy.15 = bf16[128,512]{1,0:T(8,128)(2,1)} copy(bf16[128,512]{1,0:T(8,128)(2,1)} %get-tuple-element.13) | data formatting | bytes 262144

commit v2 on v1

--- a/solution.py
+++ b/solution.py
@@ -32,7 +32,7 @@
 def moe_kernel(
     parts, experts, cap,
     x_ref, dy_ref, p_ref, id_ref, wg_hbm, wd_hbm,
-    lo_ref, ig_ref, pg_ref,
+    both_ref, pg_ref,
     wg, wd, home, pick0, pick1, spread, weight,
     send, recv, pre, back, hid, gterm, rsend, rrecv,
     part, gathered, own, pacc, psend, precv,
@@ -64,17 +64,18 @@
             barrier, inc=1, device_id={"expert": flip(me, j, experts)}, device_id_type=MESH
         )
 
-    ids = id_ref[...]
-    probs = p_ref[...]
-    id0, id1 = ids[:, 0:1], ids[:, 1:2]
-    p0, p1 = probs[:, 0:1], probs[:, 1:2]
+    across = lax.broadcasted_iota(jnp.int32, (tokens, tokens), 1)
+    down = lax.broadcasted_iota(jnp.int32, (tokens, tokens), 0)
+
+    def column(row):
+        return jnp.sum(jnp.where(across == down, row, 0), axis=1, keepdims=True)
+
+    id0, id1 = column(id_ref[0:1, :]), column(id_ref[1:2, :])
+    p0, p1 = column(p_ref[0:1, :]), column(p_ref[1:2, :])
     lane = lax.broadcasted_iota(jnp.int32, (tokens, LANES), 1)
     hot0 = (lane == id0).astype(f32)
     hot1 = (lane == id1).astype(f32)
-    earlier = (
-        lax.broadcasted_iota(jnp.int32, (tokens, tokens), 1)
-        < lax.broadcasted_iota(jnp.int32, (tokens, tokens), 0)
-    ).astype(f32)
+    earlier = (across < down).astype(f32)
     count = nn_dot(earlier.astype(bf16), (hot0 + hot1).astype(bf16))
     pos0 = jnp.sum(count * hot0, axis=1, keepdims=True)
     pos1 = jnp.sum(count * hot1, axis=1, keepdims=True)
@@ -92,7 +93,8 @@
     back[...] = jnp.zeros_like(back)
     pacc[...] = jnp.zeros_like(pacc)
 
-    pl.semaphore_wait(barrier, parts - 1 + experts - 1)
+    with jax.named_scope("entry"):
+        pl.semaphore_wait(barrier, parts - 1 + experts - 1)
 
     def to_home(i):
         peer = flip(z, i, parts)
@@ -133,13 +135,16 @@
         send[chunk, :, cap:] = gs.reshape(experts, cap, cols)
         exchange(send, recv, chunk, a_send, a_recv, loc_sem)
 
-    dispatch(z)
+    with jax.named_scope("dispatch_own"):
+        dispatch(z)
 
     @pl.loop(1, parts)
     def _(i):
         chunk = flip(z, i, parts)
-        pltpu.make_async_copy(home.at[chunk], home.at[chunk], ag_recv.at[chunk]).wait()
-        dispatch(chunk)
+        with jax.named_scope("home_wait"):
+            pltpu.make_async_copy(home.at[chunk], home.at[chunk], ag_recv.at[chunk]).wait()
+        with jax.named_scope("dispatch"):
+            dispatch(chunk)
 
     load_g.wait()
     load_d.wait()
@@ -148,29 +153,32 @@
     def _(i):
         chunk = flip(z, i, parts)
         start = pl.multiple_of(chunk * cols, cols)
-        exchanged(send, recv, chunk, a_send, a_recv, loc_sem)
+        with jax.named_scope("rows_wait"):
+            exchanged(send, recv, chunk, a_send, a_recv, loc_sem)
         xr = recv[chunk, :, 0:cap].reshape(rows, cols)
         gr = recv[chunk, :, cap:].reshape(rows, cols)
-        pre[...] += nn_dot(xr, wg[pl.ds(start, cols), :])
+        pre[...] += nt_dot(xr, wg[:, pl.ds(start, cols)])
         back[...] += nt_dot(gr, wd[:, pl.ds(start, cols)])
 
-    v = pre[...]
-    sig = jax.nn.sigmoid(v)
-    hid[...] = (v * sig).astype(bf16)
-    gterm[...] = (back[...] * sig * (1.0 + v * (1.0 - sig))).astype(bf16)
+    with jax.named_scope("activation"):
+        v = pre[...]
+        sig = jax.nn.sigmoid(v)
+        hid[...] = (v * sig).astype(bf16)
+        gterm[...] = (back[...] * sig * (1.0 + v * (1.0 - sig))).astype(bf16)
 
     @pl.loop(1, parts + 1)
     def _(i):
         chunk = flip(z, i % parts, parts)
         start = pl.multiple_of(chunk * cols, cols)
         out = nn_dot(hid[...], wd[:, pl.ds(start, cols)]).astype(bf16)
-        grad = nt_dot(gterm[...], wg[pl.ds(start, cols), :]).astype(bf16)
+        grad = nn_dot(gterm[...], wg[:, pl.ds(start, cols)]).astype(bf16)
         rsend[chunk, :, 0:cap] = out.reshape(experts, cap, cols)
         rsend[chunk, :, cap:] = grad.reshape(experts, cap, cols)
         exchange(rsend, rrecv, chunk, r_send, r_recv, rloc_sem)
 
     def combine(chunk):
-        exchanged(rsend, rrecv, chunk, r_send, r_recv, rloc_sem)
+        with jax.named_scope("back_wait"):
+            exchanged(rsend, rrecv, chunk, r_send, r_recv, rloc_sem)
         out = rrecv[chunk, :, 0:cap].reshape(rows, cols)
         grad = rrecv[chunk, :, cap:].reshape(rows, cols)
         out0, out1 = nn_dot(pick0[...], out), nn_dot(pick1[...], out)
@@ -178,8 +186,7 @@
         s0 = jnp.sum(dy * out0, axis=1, keepdims=True)
         s1 = jnp.sum(dy * out1, axis=1, keepdims=True)
         pacc[...] += jnp.where(lane == 0, s0, 0.0) + jnp.where(lane == 1, s1, 0.0)
-        weights = p_ref[...]
-        layer = weights[:, 0:1] * out0 + weights[:, 1:2] * out1
+        layer = p0 * out0 + p1 * out1
         return layer, nn_dot(pick0[...] + pick1[...], grad)
 
     def to_owner(chunk):
@@ -211,23 +218,24 @@
         ).start()
 
     others = gathered.at[pl.ds(0, parts - 1)]
-    pltpu.make_async_copy(others, others, s_recv).wait()
+    with jax.named_scope("sums_wait"):
+        pltpu.make_async_copy(others, others, s_recv).wait()
 
     @pl.loop(1, parts)
     def _(i):
         other = flip(z, i, parts)
         own[...] += gathered[other].astype(f32)
 
-    lo_ref[...] = own[0].astype(bf16)
-    ig_ref[...] = own[1].astype(bf16)
+    both_ref[...] = own[...].astype(bf16)
 
     rest = precv.at[pl.ds(0, parts - 1)]
-    pltpu.make_async_copy(rest, rest, p_recv).wait()
-    pg_ref[...] = psend[...]
-
-    @pl.loop(1, parts)
-    def _(i):
-        pg_ref[...] += precv[flip(z, i, parts)]
+    with jax.named_scope("prob_wait"):
+        pltpu.make_async_copy(rest, rest, p_recv).wait()
+    pg_ref[...] = psend[0:2]
+
+    @pl.loop(1, parts)
+    def _(i):
+        pg_ref[...] += precv[flip(z, i, parts), 0:2]
 
     sent = home.at[pl.ds(0, parts - 1)]
     pltpu.make_async_copy(sent, sent, ag_send).wait()
@@ -239,6 +247,12 @@
     def _(i):
         pltpu.make_async_copy(several, several, a_send).wait()
         pltpu.make_async_copy(several, several, r_send).wait()
+
+
+def split_kernel(both_ref, prob_ref, lo_ref, ig_ref, pg_ref):
+    lo_ref[...] = both_ref[0]
+    ig_ref[...] = both_ref[1]
+    pg_ref[...] = prob_ref[...]
 
 
 def per_device(inputs, out_grad, gate_probs, expert_ids, gate_proj, down_proj):
@@ -252,17 +266,16 @@
     vmem = pl.BlockSpec(memory_space=pltpu.VMEM)
     hbm = pl.BlockSpec(memory_space=pl.ANY)
     dma = pltpu.SemaphoreType.DMA
-    layer_out, in_grad, prob = pl.pallas_call(
+    both, prob = pl.pallas_call(
         functools.partial(moe_kernel, parts, experts, cap),
         out_shape=(
-            jax.ShapeDtypeStruct((tokens, cols), bf16),
-            jax.ShapeDtypeStruct((tokens, cols), bf16),
-            jax.ShapeDtypeStruct((8, tokens), f32),
+            jax.ShapeDtypeStruct((2, tokens, cols), bf16),
+            jax.ShapeDtypeStruct((2, tokens), f32),
         ),
         in_specs=[vmem, vmem, vmem, vmem, hbm, hbm],
-        out_specs=(vmem, vmem, vmem),
+        out_specs=(vmem, vmem),
         scratch_shapes=[
-            pltpu.VMEM((width, hidden), bf16),
+            pltpu.VMEM((hidden, width), bf16),
             pltpu.VMEM((hidden, width), bf16),
             pltpu.VMEM((parts, 2, tokens, cols), bf16),
             pltpu.VMEM((tokens, rows), bf16),
@@ -289,8 +302,18 @@
         compiler_params=pltpu.CompilerParams(
             collective_id=0, has_side_effects=True, vmem_limit_bytes=56 * 1024 * 1024
         ),
-    )(inputs, out_grad, gate_probs, expert_ids, gate_proj, down_proj)
-    return layer_out, in_grad, prob[:2].T
+    )(inputs, out_grad, gate_probs.T, expert_ids.T, jnp.swapaxes(gate_proj, 1, 2), down_proj)
+    layer_out, in_grad, prob_grad = pl.pallas_call(
+        split_kernel,
+        out_shape=(
+            jax.ShapeDtypeStruct((tokens, cols), bf16),
+            jax.ShapeDtypeStruct((tokens, cols), bf16),
+            jax.ShapeDtypeStruct((2, tokens), f32),
+        ),
+        in_specs=[vmem, vmem],
+        out_specs=(vmem, vmem, vmem),
+    )(both, prob)
+    return layer_out, in_grad, prob_grad.T
 
 
 def solution(mesh):

time: 103 us -> 92.5 us (0.90)
  local copies, waits for them, and re-layouts: 11.5 us -> 0 us
  Pallas kernels: 90.1 us -> 91.7 us
    unnamed x5 -> x0, local copies, waits for them, and re-layouts: 10.3 us -> none
    pallas_call x0 -> x1, Pallas kernels: none -> 1.66 us  [per_device(): pl.pallas_call(split_kernel, out_shape=(jax.ShapeDtypeStruct((tokens, col...]
    transpose x1 -> x0, local copies, waits for them, and re-layouts: 1.24 us -> none  [per_device(): return (layer_out, in_grad, prob[:2].T)]
where the time goes in v2:
time: 92.5 us; the launch traced here: 92.4 us
  Pallas kernels  91.7 us (99%)
    pallas_call x1, Pallas kernels, per_device(): pl.pallas_call(functools.partial(moe_kernel, parts, experts, cap), out_sh...  90.1 us

profile of v2, /device:TPU:0, one launch (start us, length us, event | category | flops | bytes accessed | tf_op | source)
XLA Modules:
  0.0 92.4 jit_solution(811755199212377265)
XLA Ops:
  0.6 90.1 %shard_map.85 = (bf16[2,128,512]{2,1,0:T(8,128)(2,1)}, f32[2,128]{1,0:T(2,128)}) custom-call(bf16[128,512]{1,0:T(8,128)(2,1)} %x_ref.1, bf16[128,512]{1,0:T(8,128)(2,1)} %dy_ref.1, f32[2,128]{1,0:T(2,128)} %bitcast.5, s32[2,128]{1,0:T(2,128)} %bitcast.6, bf16[1,576,2048]{2,1,0:T(8,128)(2,1)} %bitcast.4, bf16[1,576,2048]{2,1,0:T(8,128)(2,1)} %wd_hbm.1), custom_call_target="tpu_custom_call" | custom-call | tf_op jit(solution)/shard_map/pallas_call | solution.py:269
  90.7 1.7 %shard_map.86 = (bf16[128,512]{1,0:T(8,128)(2,1)}, bf16[128,512]{1,0:T(8,128)(2,1)}, f32[2,128]{1,0:T(2,128)}) custom-call(bf16[2,128,512]{2,1,0:T(8,128)(2,1)} %get-tuple-element.8.both_ref, f32[2,128]{1,0:T(2,128)} %get-tuple-element.9.prob_ref), custom_call_target="tpu_custom_call" | custom-call | tf_op jit(solution)/shard_map/pallas_call | solution.py:306

commit v3 on v2

--- a/solution.py
+++ b/solution.py
@@ -35,12 +35,14 @@
     both_ref, pg_ref,
     wg, wd, home, pick0, pick1, spread, weight,
     send, recv, pre, back, hid, gterm, rsend, rrecv,
-    part, gathered, own, pacc, psend, precv,
+    part, gathered, own, pacc, psend, precv, fsum, fsend,
     w_sem, ag_send, ag_recv, loc_sem, a_send, a_recv, rloc_sem, r_send, r_recv,
-    s_send, s_recv, p_send, p_recv,
+    s_send, s_recv, p_send, p_recv, f_send, f_recv, g_send, g_recv, h_send, h_recv,
+    k_send,
 ):
     z = lax.axis_index("dp")
     me = lax.axis_index("expert")
+    far = flip(me, experts - 2, experts)
     tokens, cols = x_ref.shape
     rows = experts * cap
     bf16, f32 = jnp.bfloat16, jnp.float32
@@ -93,6 +95,10 @@
     back[...] = jnp.zeros_like(back)
     pacc[...] = jnp.zeros_like(pacc)
 
+    @pl.loop(1, parts)
+    def _(i):
+        rrecv[flip(z, i, parts), far] = jnp.zeros((2 * cap, cols), bf16)
+
     with jax.named_scope("entry"):
         pl.semaphore_wait(barrier, parts - 1 + experts - 1)
 
@@ -109,56 +115,89 @@
         to_home(i).start()
 
     def exchange(source, target, chunk, send_sem, recv_sem, local_sem):
-        @pl.loop(1, experts)
-        def _(j):
-            peer = flip(me, experts - j, experts)
+        def put(j):
+            peer = flip(me, j, experts)
             pltpu.make_async_remote_copy(
                 src_ref=source.at[chunk, peer], dst_ref=target.at[chunk, me],
                 send_sem=send_sem, recv_sem=recv_sem.at[chunk],
                 device_id={"expert": peer}, device_id_type=MESH,
             ).start()
+
+        put(experts - 1)
+
+        @pl.loop(3, experts)
+        def _(j):
+            put(experts - j)
+
         pltpu.make_async_copy(
             source.at[chunk, me], target.at[chunk, me], local_sem.at[chunk]
         ).start()
 
-    def exchanged(source, target, chunk, send_sem, recv_sem, local_sem):
+    def exchanged(source, target, chunk, blocks, recv_sem, local_sem):
         pltpu.make_async_copy(
             source.at[chunk, me], target.at[chunk, me], local_sem.at[chunk]
         ).wait()
-        several = target.at[chunk, pl.ds(0, experts - 1)]
+        several = target.at[chunk, pl.ds(0, blocks)]
         pltpu.make_async_copy(several, several, recv_sem.at[chunk]).wait()
 
-    def dispatch(chunk):
+    def slot_rows(chunk):
         xs = nn_dot(spread[...], home[chunk, 0]).astype(bf16)
         gs = (weight[...] * nn_dot(spread[...], home[chunk, 1])).astype(bf16)
         send[chunk, :, 0:cap] = xs.reshape(experts, cap, cols)
         send[chunk, :, cap:] = gs.reshape(experts, cap, cols)
+
+    slot_rows(z)
+    pltpu.make_async_remote_copy(
+        src_ref=send.at[z, far], dst_ref=recv.at[z, me],
+        send_sem=f_send, recv_sem=f_recv,
+        device_id={"expert": far}, device_id_type=MESH,
+    ).start()
+    exchange(send, recv, z, a_send, a_recv, loc_sem)
+
+    def dispatch(i):
+        chunk = flip(z, i, parts)
+        pltpu.make_async_copy(home.at[chunk], home.at[chunk], ag_recv.at[chunk]).wait()
+        slot_rows(chunk)
         exchange(send, recv, chunk, a_send, a_recv, loc_sem)
 
-    with jax.named_scope("dispatch_own"):
-        dispatch(z)
-
-    @pl.loop(1, parts)
-    def _(i):
-        chunk = flip(z, i, parts)
-        with jax.named_scope("home_wait"):
-            pltpu.make_async_copy(home.at[chunk], home.at[chunk], ag_recv.at[chunk]).wait()
-        with jax.named_scope("dispatch"):
-            dispatch(chunk)
+    @pl.loop(1, parts - 0)
+    def _(i):
+        dispatch(i)
+
+    block = recv.at[z, far]
+    pltpu.make_async_copy(block, block, f_recv).wait()
+
+    @pl.loop(1, parts)
+    def _(i):
+        pltpu.make_async_remote_copy(
+            src_ref=recv.at[z, far], dst_ref=recv.at[z, far],
+            send_sem=g_send, recv_sem=g_recv.at[z],
+            device_id={"dp": flip(z, i, parts)}, device_id_type=MESH,
+        ).start()
+
+    @pl.loop(parts - 0, parts)
+    def _(i):
+        dispatch(i)
 
     load_g.wait()
     load_d.wait()
 
-    @pl.loop(0, parts)
-    def _(i):
-        chunk = flip(z, i, parts)
+    def contract(chunk):
         start = pl.multiple_of(chunk * cols, cols)
-        with jax.named_scope("rows_wait"):
-            exchanged(send, recv, chunk, a_send, a_recv, loc_sem)
+        exchanged(send, recv, chunk, experts - 2, a_recv, loc_sem)
         xr = recv[chunk, :, 0:cap].reshape(rows, cols)
         gr = recv[chunk, :, cap:].reshape(rows, cols)
         pre[...] += nt_dot(xr, wg[:, pl.ds(start, cols)])
         back[...] += nt_dot(gr, wd[:, pl.ds(start, cols)])
+
+    contract(z)
+
+    @pl.loop(1, parts)
+    def _(i):
+        chunk = flip(z, i, parts)
+        relayed = recv.at[chunk, far]
+        pltpu.make_async_copy(relayed, relayed, g_recv.at[chunk]).wait()
+        contract(chunk)
 
     with jax.named_scope("activation"):
         v = pre[...]
@@ -166,19 +205,40 @@
         hid[...] = (v * sig).astype(bf16)
         gterm[...] = (back[...] * sig * (1.0 + v * (1.0 - sig))).astype(bf16)
 
-    @pl.loop(1, parts + 1)
-    def _(i):
-        chunk = flip(z, i % parts, parts)
+    def produce(chunk):
         start = pl.multiple_of(chunk * cols, cols)
         out = nn_dot(hid[...], wd[:, pl.ds(start, cols)]).astype(bf16)
         grad = nn_dot(gterm[...], wg[:, pl.ds(start, cols)]).astype(bf16)
         rsend[chunk, :, 0:cap] = out.reshape(experts, cap, cols)
         rsend[chunk, :, cap:] = grad.reshape(experts, cap, cols)
+
+    @pl.loop(1, parts)
+    def _(i):
+        chunk = flip(z, parts - i, parts)
+        produce(chunk)
+        pltpu.make_async_remote_copy(
+            src_ref=rsend.at[chunk, far], dst_ref=fsum.at[z],
+            send_sem=h_send, recv_sem=h_recv,
+            device_id={"dp": chunk}, device_id_type=MESH,
+        ).start()
         exchange(rsend, rrecv, chunk, r_send, r_recv, rloc_sem)
 
-    def combine(chunk):
-        with jax.named_scope("back_wait"):
-            exchanged(rsend, rrecv, chunk, r_send, r_recv, rloc_sem)
+    produce(z)
+    exchange(rsend, rrecv, z, r_send, r_recv, rloc_sem)
+    sums = fsum.at[pl.ds(0, parts - 1)]
+    pltpu.make_async_copy(sums, sums, h_recv).wait()
+    fsend[...] = lax.fori_loop(
+        1, parts, lambda i, total: total + fsum[flip(z, i, parts)].astype(f32),
+        rsend[z, far].astype(f32),
+    ).astype(bf16)
+    pltpu.make_async_remote_copy(
+        src_ref=fsend, dst_ref=rrecv.at[z, me],
+        send_sem=k_send, recv_sem=r_recv.at[z],
+        device_id={"expert": far}, device_id_type=MESH,
+    ).start()
+
+    def combine(chunk, blocks):
+        exchanged(rsend, rrecv, chunk, blocks, r_recv, rloc_sem)
         out = rrecv[chunk, :, 0:cap].reshape(rows, cols)
         grad = rrecv[chunk, :, cap:].reshape(rows, cols)
         out0, out1 = nn_dot(pick0[...], out), nn_dot(pick1[...], out)
@@ -198,13 +258,13 @@
 
     @pl.loop(1, parts)
     def _(i):
-        chunk = flip(z, i, parts)
-        layer, grad = combine(chunk)
+        chunk = flip(z, parts - i, parts)
+        layer, grad = combine(chunk, experts - 2)
         part[chunk, 0] = layer.astype(bf16)
         part[chunk, 1] = grad.astype(bf16)
         to_owner(chunk).start()
 
-    layer, grad = combine(z)
+    layer, grad = combine(z, experts - 1)
     own[0] = layer
     own[1] = grad
     psend[...] = jnp.transpose(pacc[...])[0:8]
@@ -241,12 +301,17 @@
     pltpu.make_async_copy(sent, sent, ag_send).wait()
     pltpu.make_async_copy(others, others, s_send).wait()
     pltpu.make_async_copy(rest, rest, p_send).wait()
-    several = send.at[0, pl.ds(0, experts - 1)]
+    several = send.at[0, pl.ds(0, experts - 2)]
 
     @pl.loop(0, parts)
     def _(i):
         pltpu.make_async_copy(several, several, a_send).wait()
         pltpu.make_async_copy(several, several, r_send).wait()
+
+    pltpu.make_async_copy(fsend, fsend, f_send).wait()
+    pltpu.make_async_copy(fsend, fsend, k_send).wait()
+    pltpu.make_async_copy(sums, sums, g_send).wait()
+    pltpu.make_async_copy(sums, sums, h_send).wait()
 
 
 def split_kernel(both_ref, prob_ref, lo_ref, ig_ref, pg_ref):
@@ -296,8 +361,11 @@
             pltpu.VMEM((tokens, LANES), f32),
             pltpu.VMEM((8, tokens), f32),
             pltpu.VMEM((parts, 8, tokens), f32),
+            pltpu.VMEM((parts, 2 * cap, cols), bf16),
+            pltpu.VMEM((2 * cap, cols), bf16),
             dma((2,)), dma, dma((parts,)), dma((parts,)), dma, dma((parts,)),
             dma((parts,)), dma, dma((parts,)), dma, dma, dma, dma,
+            dma, dma, dma, dma((parts,)), dma, dma, dma,
         ],
         compiler_params=pltpu.CompilerParams(
             collective_id=0, has_side_effects=True, vmem_limit_bytes=56 * 1024 * 1024

time: 92.5 us -> 81.7 us (0.88)
  Pallas kernels: 91.7 us -> 80.9 us
    pallas_call x1, Pallas kernels: 90.1 us -> 79.2 us  [per_device(): pl.pallas_call(functools.partial(moe_kernel, parts, experts, cap), out_sh...]
where the time goes in v3:
time: 81.7 us; the launch traced here: 81.5 us
  Pallas kernels  80.9 us (99%)
    pallas_call x1, Pallas kernels, per_device(): pl.pallas_call(functools.partial(moe_kernel, parts, experts, cap), out_sh...  79.2 us
    pallas_call x1, Pallas kernels, per_device(): pl.pallas_call(split_kernel, out_shape=(jax.ShapeDtypeStruct((tokens, col...  1.66 us

profile of v3, /device:TPU:0, one launch (start us, length us, event | category | flops | bytes accessed | tf_op | source)
XLA Modules:
  0.0 81.5 jit_solution(11955725481153404060)
XLA Ops:
  0.6 79.2 %shard_map.85 = (bf16[2,128,512]{2,1,0:T(8,128)(2,1)}, f32[2,128]{1,0:T(2,128)}) custom-call(bf16[128,512]{1,0:T(8,128)(2,1)} %x_ref.1, bf16[128,512]{1,0:T(8,128)(2,1)} %dy_ref.1, f32[2,128]{1,0:T(2,128)} %bitcast.5, s32[2,128]{1,0:T(2,128)} %bitcast.6, bf16[1,576,2048]{2,1,0:T(8,128)(2,1)} %bitcast.4, bf16[1,576,2048]{2,1,0:T(8,128)(2,1)} %wd_hbm.1), custom_call_target="tpu_custom_call" | custom-call | tf_op jit(solution)/shard_map/pallas_call | solution.py:334
  79.8 1.7 %shard_map.86 = (bf16[128,512]{1,0:T(8,128)(2,1)}, bf16[128,512]{1,0:T(8,128)(2,1)}, f32[2,128]{1,0:T(2,128)}) custom-call(bf16[2,128,512]{2,1,0:T(8,128)(2,1)} %get-tuple-element.8.both_ref, f32[2,128]{1,0:T(2,128)} %get-tuple-element.9.prob_ref), custom_call_target="tpu_custom_call" | custom-call | tf_op jit(solution)/shard_map/pallas_call | solution.py:374

commit v4 on v3

--- a/solution.py
+++ b/solution.py
@@ -102,17 +102,22 @@
     with jax.named_scope("entry"):
         pl.semaphore_wait(barrier, parts - 1 + experts - 1)
 
-    def to_home(i):
-        peer = flip(z, i, parts)
+    rightward, leftward = z + 1 < parts, z > 0
+
+    def pass_on(shard, neighbour):
         return pltpu.make_async_remote_copy(
-            src_ref=home.at[z], dst_ref=home.at[z],
-            send_sem=ag_send, recv_sem=ag_recv.at[z],
-            device_id={"dp": peer}, device_id_type=MESH,
+            src_ref=home.at[shard], dst_ref=home.at[shard],
+            send_sem=ag_send, recv_sem=ag_recv.at[shard],
+            device_id={"dp": neighbour}, device_id_type=MESH,
         )
 
-    @pl.loop(1, parts)
-    def _(i):
-        to_home(i).start()
+    @pl.when(rightward)
+    def _():
+        pass_on(z, z + 1).start()
+
+    @pl.when(leftward)
+    def _():
+        pass_on(z, z - 1).start()
 
     def exchange(source, target, chunk, send_sem, recv_sem, local_sem):
         def put(j):
@@ -154,15 +159,37 @@
     ).start()
     exchange(send, recv, z, a_send, a_recv, loc_sem)
 
-    def dispatch(i):
-        chunk = flip(z, i, parts)
-        pltpu.make_async_copy(home.at[chunk], home.at[chunk], ag_recv.at[chunk]).wait()
-        slot_rows(chunk)
-        exchange(send, recv, chunk, a_send, a_recv, loc_sem)
-
-    @pl.loop(1, parts - 0)
-    def _(i):
-        dispatch(i)
+    @pl.loop(1, parts)
+    def _(i):
+        lower, upper = z - i, z + i
+
+        @pl.when(lower >= 0)
+        def _():
+            shard = home.at[lower]
+            pltpu.make_async_copy(shard, shard, ag_recv.at[lower]).wait()
+
+            @pl.when(rightward)
+            def _():
+                pass_on(lower, z + 1).start()
+
+        @pl.when(upper < parts)
+        def _():
+            shard = home.at[upper]
+            pltpu.make_async_copy(shard, shard, ag_recv.at[upper]).wait()
+
+            @pl.when(leftward)
+            def _():
+                pass_on(upper, z - 1).start()
+
+        @pl.when(lower >= 0)
+        def _():
+            slot_rows(lower)
+            exchange(send, recv, lower, a_send, a_recv, loc_sem)
+
+        @pl.when(upper < parts)
+        def _():
+            slot_rows(upper)
+            exchange(send, recv, upper, a_send, a_recv, loc_sem)
 
     block = recv.at[z, far]
     pltpu.make_async_copy(block, block, f_recv).wait()
@@ -174,10 +201,6 @@
             send_sem=g_send, recv_sem=g_recv.at[z],
             device_id={"dp": flip(z, i, parts)}, device_id_type=MESH,
         ).start()
-
-    @pl.loop(parts - 0, parts)
-    def _(i):
-        dispatch(i)
 
     load_g.wait()
     load_d.wait()
@@ -297,8 +320,20 @@
     def _(i):
         pg_ref[...] += precv[flip(z, i, parts), 0:2]
 
-    sent = home.at[pl.ds(0, parts - 1)]
-    pltpu.make_async_copy(sent, sent, ag_send).wait()
+    passed = home.at[z]
+
+    @pl.when(rightward)
+    def _():
+        @pl.loop(0, z + 1)
+        def _(i):
+            pltpu.make_async_copy(passed, passed, ag_send).wait()
+
+    @pl.when(leftward)
+    def _():
+        @pl.loop(0, parts - z)
+        def _(i):
+            pltpu.make_async_copy(passed, passed, ag_send).wait()
+
     pltpu.make_async_copy(others, others, s_send).wait()
     pltpu.make_async_copy(rest, rest, p_send).wait()
     several = send.at[0, pl.ds(0, experts - 2)]

time: 81.7 us -> 76.4 us (0.935)
  Pallas kernels: 80.9 us -> 75.6 us
    pallas_call x1, Pallas kernels: 79.2 us -> 73.9 us  [per_device(): pl.pallas_call(functools.partial(moe_kernel, parts, experts, cap), out_sh...]
where the time goes in v4:
time: 76.4 us; the launch traced here: 76.2 us
  Pallas kernels  75.6 us (99%)
    pallas_call x1, Pallas kernels, per_device(): pl.pallas_call(functools.partial(moe_kernel, parts, experts, cap), out_sh...  73.9 us
    pallas_call x1, Pallas kernels, per_device(): pl.pallas_call(split_kernel, out_shape=(jax.ShapeDtypeStruct((tokens, col...  1.66 us

profile of v4, /device:TPU:0, one launch (start us, length us, event | category | flops | bytes accessed | tf_op | source)
XLA Modules:
  0.0 76.2 jit_solution(17990780809628223318)
XLA Ops:
  0.6 73.9 %shard_map.85 = (bf16[2,128,512]{2,1,0:T(8,128)(2,1)}, f32[2,128]{1,0:T(2,128)}) custom-call(bf16[128,512]{1,0:T(8,128)(2,1)} %x_ref.1, bf16[128,512]{1,0:T(8,128)(2,1)} %dy_ref.1, f32[2,128]{1,0:T(2,128)} %bitcast.5, s32[2,128]{1,0:T(2,128)} %bitcast.6, bf16[1,576,2048]{2,1,0:T(8,128)(2,1)} %bitcast.4, bf16[1,576,2048]{2,1,0:T(8,128)(2,1)} %wd_hbm.1), custom_call_target="tpu_custom_call" | custom-call | tf_op jit(solution)/shard_map/pallas_call | solution.py:369
  74.5 1.7 %shard_map.86 = (bf16[128,512]{1,0:T(8,128)(2,1)}, bf16[128,512]{1,0:T(8,128)(2,1)}, f32[2,128]{1,0:T(2,128)}) custom-call(bf16[2,128,512]{2,1,0:T(8,128)(2,1)} %get-tuple-element.8.both_ref, f32[2,128]{1,0:T(2,128)} %get-tuple-element.9.prob_ref), custom_call_target="tpu_custom_call" | custom-call | tf_op jit(solution)/shard_map/pallas_call | solution.py:409

commit v5 on v4

--- a/solution.py
+++ b/solution.py
@@ -235,9 +235,20 @@
         rsend[chunk, :, 0:cap] = out.reshape(experts, cap, cols)
         rsend[chunk, :, cap:] = grad.reshape(experts, cap, cols)
 
-    @pl.loop(1, parts)
-    def _(i):
-        chunk = flip(z, parts - i, parts)
+    def farthest_first(body):
+        @pl.loop(1, parts)
+        def _(i):
+            lower, upper = z - (parts - i), z + (parts - i)
+
+            @pl.when(lower >= 0)
+            def _():
+                body(lower)
+
+            @pl.when(upper < parts)
+            def _():
+                body(upper)
+
+    def give_back(chunk):
         produce(chunk)
         pltpu.make_async_remote_copy(
             src_ref=rsend.at[chunk, far], dst_ref=fsum.at[z],
@@ -246,6 +257,7 @@
         ).start()
         exchange(rsend, rrecv, chunk, r_send, r_recv, rloc_sem)
 
+    farthest_first(give_back)
     produce(z)
     exchange(rsend, rrecv, z, r_send, r_recv, rloc_sem)
     sums = fsum.at[pl.ds(0, parts - 1)]
@@ -272,20 +284,42 @@
         layer = p0 * out0 + p1 * out1
         return layer, nn_dot(pick0[...] + pick1[...], grad)
 
-    def to_owner(chunk):
-        return pltpu.make_async_remote_copy(
-            src_ref=part.at[chunk], dst_ref=gathered.at[z],
-            send_sem=s_send, recv_sem=s_recv,
-            device_id={"dp": chunk}, device_id_type=MESH,
-        )
-
-    @pl.loop(1, parts)
-    def _(i):
-        chunk = flip(z, parts - i, parts)
+    def add_from(side, chunk):
+        arrived = gathered.at[side, chunk]
+        pltpu.make_async_copy(arrived, arrived, s_recv.at[side, chunk]).wait()
+        own[...] += gathered[side, chunk].astype(f32)
+
+    def hand_on(side, chunk, neighbour):
+        pltpu.make_async_remote_copy(
+            src_ref=part.at[chunk], dst_ref=gathered.at[side, chunk],
+            send_sem=s_send, recv_sem=s_recv.at[side, chunk],
+            device_id={"dp": neighbour}, device_id_type=MESH,
+        ).start()
+
+    def sum_on(chunk):
         layer, grad = combine(chunk, experts - 2)
-        part[chunk, 0] = layer.astype(bf16)
-        part[chunk, 1] = grad.astype(bf16)
-        to_owner(chunk).start()
+        own[0] = layer
+        own[1] = grad
+
+        @pl.when((chunk > z) & leftward)
+        def _():
+            add_from(0, chunk)
+
+        @pl.when((chunk < z) & rightward)
+        def _():
+            add_from(1, chunk)
+
+        part[chunk] = own[...].astype(bf16)
+
+        @pl.when(chunk > z)
+        def _():
+            hand_on(0, chunk, z + 1)
+
+        @pl.when(chunk < z)
+        def _():
+            hand_on(1, chunk, z - 1)
+
+    farthest_first(sum_on)
 
     layer, grad = combine(z, experts - 1)
     own[0] = layer
@@ -300,14 +334,13 @@
             device_id={"dp": flip(z, i, parts)}, device_id_type=MESH,
         ).start()
 
-    others = gathered.at[pl.ds(0, parts - 1)]
-    with jax.named_scope("sums_wait"):
-        pltpu.make_async_copy(others, others, s_recv).wait()
-
-    @pl.loop(1, parts)
-    def _(i):
-        other = flip(z, i, parts)
-        own[...] += gathered[other].astype(f32)
+    @pl.when(leftward)
+    def _():
+        add_from(0, z)
+
+    @pl.when(rightward)
+    def _():
+        add_from(1, z)
 
     both_ref[...] = own[...].astype(bf16)
 
@@ -334,6 +367,7 @@
         def _(i):
             pltpu.make_async_copy(passed, passed, ag_send).wait()
 
+    others = part.at[pl.ds(0, parts - 1)]
     pltpu.make_async_copy(others, others, s_send).wait()
     pltpu.make_async_copy(rest, rest, p_send).wait()
     several = send.at[0, pl.ds(0, experts - 2)]
@@ -391,7 +425,7 @@
             pltpu.VMEM((parts, experts, 2 * cap, cols), bf16),
             pltpu.VMEM((parts, experts, 2 * cap, cols), bf16),
             pltpu.VMEM((parts, 2, tokens, cols), bf16),
-            pltpu.VMEM((parts, 2, tokens, cols), bf16),
+            pltpu.VMEM((2, parts, 2, tokens, cols), bf16),
             pltpu.VMEM((2, tokens, cols), f32),
             pltpu.VMEM((tokens, LANES), f32),
             pltpu.VMEM((8, tokens), f32),
@@ -399,7 +433,7 @@
             pltpu.VMEM((parts, 2 * cap, cols), bf16),
             pltpu.VMEM((2 * cap, cols), bf16),
             dma((2,)), dma, dma((parts,)), dma((parts,)), dma, dma((parts,)),
-            dma((parts,)), dma, dma((parts,)), dma, dma, dma, dma,
+            dma((parts,)), dma, dma((parts,)), dma, dma((2, parts)), dma, dma,
             dma, dma, dma, dma((parts,)), dma, dma, dma,
         ],
         compiler_params=pltpu.CompilerParams(

time: 76.4 us -> 74.6 us (0.976)
  Pallas kernels: 75.6 us -> 73.8 us
    pallas_call x1, Pallas kernels: 73.9 us -> 72.1 us  [per_device(): pl.pallas_call(functools.partial(moe_kernel, parts, experts, cap), out_sh...]
where the time goes in v5:
time: 74.6 us; the launch traced here: 74.4 us
  Pallas kernels  73.8 us (99%)
    pallas_call x1, Pallas kernels, per_device(): pl.pallas_call(functools.partial(moe_kernel, parts, experts, cap), out_sh...  72.1 us
    pallas_call x1, Pallas kernels, per_device(): pl.pallas_call(split_kernel, out_shape=(jax.ShapeDtypeStruct((tokens, col...  1.66 us

profile of v5, /device:TPU:0, one launch (start us, length us, event | category | flops | bytes accessed | tf_op | source)
XLA Modules:
  0.0 74.4 jit_solution(16484153025065196234)
XLA Ops:
  0.6 72.1 %shard_map.85 = (bf16[2,128,512]{2,1,0:T(8,128)(2,1)}, f32[2,128]{1,0:T(2,128)}) custom-call(bf16[128,512]{1,0:T(8,128)(2,1)} %x_ref.1, bf16[128,512]{1,0:T(8,128)(2,1)} %dy_ref.1, f32[2,128]{1,0:T(2,128)} %bitcast.5, s32[2,128]{1,0:T(2,128)} %bitcast.6, bf16[1,576,2048]{2,1,0:T(8,128)(2,1)} %bitcast.4, bf16[1,576,2048]{2,1,0:T(8,128)(2,1)} %wd_hbm.1), custom_call_target="tpu_custom_call" | custom-call | tf_op jit(solution)/shard_map/pallas_call | solution.py:403
  72.8 1.7 %shard_map.86 = (bf16[128,512]{1,0:T(8,128)(2,1)}, bf16[128,512]{1,0:T(8,128)(2,1)}, f32[2,128]{1,0:T(2,128)}) custom-call(bf16[2,128,512]{2,1,0:T(8,128)(2,1)} %get-tuple-element.8.both_ref, f32[2,128]{1,0:T(2,128)} %get-tuple-element.9.prob_ref), custom_call_target="tpu_custom_call" | custom-call | tf_op jit(solution)/shard_map/pallas_call | solution.py:443
